TPU v7x, 128 devices: a whole 4x4x4 slice. The times are simulated.
128 devices in a mesh: seq: 16 (over z, x), ctx: 8 (over y, core).
Axes of the slice: x: 4, y: 4, z: 4, core: 2. Of those that a mesh axis runs over, the one named last changes fastest.
Arguments:
- queries: bfloat16 [8192, 4096], P(('seq', 'ctx')), may hold values from -90 to 90
- stretch_kv: bfloat16 [2, 8192, 1024], P(None, ('seq', 'ctx')), may hold values from -4.1 to 4.1
- cache_kv: bfloat16 [1024, 2, 8, 128, 128], P('ctx', None, None, 'seq'), may hold values from -4 to 4
- vertical: int32 [32, 8], replicated, may hold values from 0 to 1023, as said below
- slash: int32 [32, 24], replicated, may hold values from 0 to 1023
- owner_map: int32 [1024], replicated, may hold values from 0 to 1023, as said below
Outputs:
- attended: bfloat16 [8192, 4096], P(('seq', 'ctx'))
Inputs may be any that keep to these rules, and one draw needn't show every extreme that they name: For every head the 8 vertical blocks and the blocks 1024 - 1 - s of its slash entries s are 32 distinct blocks; for every head exactly 12 of them have storage rows in one range g * 128 to (g + 1) * 128 - 1, and at most 3 in each other such range, with exactly 3 in some. `owner_map`: each storage row appears once.
All inputs are finite; a program needn't handle non-finite values.
Results may differ from a plain program's by a relative error of at most 0.0075.
Values may be sent and summed in bfloat16 or wider, within the bound.
A program may use at most 128 MiB of HBM per device.

v0:
```python
import jax
import jax.numpy as jnp
from jax import lax
from jax.sharding import PartitionSpec as P

H = 32
KVH = 8
HD = 128
BLK = 128
CAP = 12
masked_value = -1e30


def stretch_positions(rows, shard, tok_rows, n_ctx):
    return (rows // tok_rows * n_ctx + shard) * tok_rows + rows % tok_rows


def online_update(carry, scores, visible, mixing):
    running_max, running_sum, weighted = carry
    masked = jnp.where(visible, scores, masked_value)
    new_max = jnp.maximum(running_max, jnp.max(masked, axis=2, keepdims=True))
    weights = jnp.where(visible, jnp.exp(masked - new_max), 0.0)
    fading = jnp.exp(running_max - new_max)
    new_sum = running_sum * fading + jnp.sum(weights, axis=2, keepdims=True)
    new_weighted = weighted * fading + mixing(weights.astype(jnp.bfloat16))
    return (new_max, new_sum, new_weighted)


def owner_slots(owner, local_row, owner_group):
    owned = owner == owner_group
    slot_rank = jnp.cumsum(owned.astype(jnp.int32), axis=1) - 1
    slot_hit = owned[:, :, None] & (
        slot_rank[:, :, None] == jnp.arange(CAP, dtype=jnp.int32)[None, None, :]
    )
    slot_row = jnp.sum(jnp.where(slot_hit, local_row[:, :, None], 0), axis=1)
    return (slot_row, jnp.any(slot_hit, axis=1))


def on_device(queries, stretch_kv, cache_kv, vertical, slash, owner_map):
    n_seq = lax.axis_size("seq")
    n_ctx = lax.axis_size("ctx")
    seq_index = lax.axis_index("seq")
    ctx_index = lax.axis_index("ctx")
    tok_rows = queries.shape[0]
    per_device = H // n_seq
    query_rows = tok_rows * n_seq
    score_scale = HD ** (-0.5)
    sent_queries = queries.reshape(tok_rows, n_seq, per_device * HD)
    own_queries = lax.all_to_all(
        sent_queries, "seq", split_axis=1, concat_axis=0, tiled=True
    ).reshape(query_rows, per_device, HD)
    widened_kv = jnp.repeat(stretch_kv.reshape(2, tok_rows, KVH, HD), n_seq // KVH, axis=2)
    own_kv = lax.all_to_all(widened_kv, "seq", split_axis=2, concat_axis=1, tiled=True).reshape(
        2, query_rows, HD
    )
    row_index = jnp.arange(query_rows, dtype=jnp.int32)
    query_position = stretch_positions(row_index, ctx_index, tok_rows, n_ctx)
    start_carry = (
        jnp.full((per_device, query_rows, 1), masked_value, jnp.float32),
        jnp.zeros((per_device, query_rows, 1), jnp.float32),
        jnp.zeros((per_device, query_rows, HD), jnp.float32),
    )
    piece = lax.all_gather(own_kv, "ctx", axis=1, tiled=True)

    def visit(index, inner):
        shard_kv = lax.dynamic_slice_in_dim(piece, index * query_rows, query_rows, 1)
        key_position = stretch_positions(row_index, index, tok_rows, n_ctx)
        scores = (
            jnp.einsum("qpd,kd->pqk", own_queries, shard_kv[0], preferred_element_type=jnp.float32)
            * score_scale
        )
        visible = (key_position[None, :] <= query_position[:, None])[None]

        def stretch_mix(rounded):
            return jnp.einsum(
                "pqk,kd->pqd", rounded, shard_kv[1], preferred_element_type=jnp.float32
            )

        return online_update(inner, scores, visible, stretch_mix)

    carry = lax.fori_loop(0, piece.shape[1] // query_rows, visit, start_carry)
    blk_ctx = cache_kv.shape[0]
    part_rows = cache_kv.shape[3]
    total_blocks = blk_ctx * n_ctx
    selected = jnp.concatenate([vertical, total_blocks - 1 - slash], axis=1)
    storage = owner_map[selected]
    owner = storage // blk_ctx
    local_row = storage % blk_ctx
    send_rows, send_hit = owner_slots(owner, local_row, ctx_index)
    head_kv = jnp.arange(H, dtype=jnp.int32) // (H // KVH)

    def group_valid(owner_group):
        return owner_slots(owner, local_row, owner_group)[1]

    valid_all = jax.vmap(group_valid)(jnp.arange(n_ctx, dtype=jnp.int32))
    own_valid = lax.dynamic_slice_in_dim(valid_all, seq_index * per_device, per_device, 1)
    packed = cache_kv[send_rows, :, head_kv[:, None]]
    packed = packed.reshape(n_seq, per_device, CAP, 2, part_rows, HD)
    widened = jnp.broadcast_to(packed[:, None], (n_seq, n_ctx) + packed.shape[1:]).reshape(
        (n_seq * n_ctx, 1) + packed.shape[1:]
    )
    received = lax.all_to_all(widened, ("seq", "ctx"), split_axis=0, concat_axis=1, tiled=True)
    arranged = received.reshape((n_seq, n_ctx) + packed.shape[1:])
    arranged = jnp.transpose(arranged, (2, 1, 3, 4, 0, 5, 6)).reshape(
        per_device, n_ctx * CAP, 2, BLK, HD
    )
    fold_piece = arranged

    def visit(index, inner):
        blocks = lax.dynamic_slice_in_dim(fold_piece, index * CAP, CAP, 1)
        owner_group = 0 // CAP + index
        live_slots = lax.dynamic_index_in_dim(own_valid, owner_group, 0, keepdims=False)
        block_keys = blocks[:, :, 0].reshape(per_device, CAP * BLK, HD)
        block_values = blocks[:, :, 1].reshape(per_device, CAP * BLK, HD)
        scores = (
            jnp.einsum("qpd,pkd->pqk", own_queries, block_keys, preferred_element_type=jnp.float32)
            * score_scale
        )
        visible = jnp.repeat(live_slots, BLK, axis=1)[:, None, :]

        def block_mix(rounded):
            return jnp.einsum(
                "pqk,pkd->pqd", rounded, block_values, preferred_element_type=jnp.float32
            )

        return online_update(inner, scores, visible, block_mix)

    carry = lax.fori_loop(0, fold_piece.shape[1] // CAP, visit, carry)
    running_max, running_sum, weighted = carry
    attended = (weighted / running_sum).astype(jnp.bfloat16)
    outgoing = jnp.transpose(attended, (1, 0, 2)).reshape(n_seq, tok_rows, per_device * HD)
    returned = lax.all_to_all(outgoing, "seq", split_axis=0, concat_axis=2, tiled=True)
    return returned.reshape(tok_rows, H * HD)


def solution(mesh):
    placed = (
        P(("seq", "ctx"), None),
        P(None, ("seq", "ctx"), None),
        P("ctx", None, None, "seq", None),
        P(),
        P(),
        P(),
    )
    return jax.shard_map(
        on_device, mesh=mesh, in_specs=placed, out_specs=P(("seq", "ctx"), None), check_vma=False
    )
```

profile of v0, /device:TPU:9, one launch (start us, length us, event | category | flops | bytes accessed | tf_op | source)
XLA Modules:
  0.0 366.4 jit_solution(12740948286434524157)
XLA Ops:
  7.7 17.9 %all_to_all.54 = bf16[2,64,16,128]{3,1,0,2:T(8,128)(2,1)S(1)} all-to-all(bf16[2,64,16,128]{3,1,0,2:T(8,128)(2,1)S(1)} %bitcast.179), channel_id=1, replica_groups=mesh['seq'=16,'ctx'=8] {'seq'}, dimensions={2} | all-to-all | bytes 1048576 | tf_op jit(solution)/shard_map/all_to_all | solution.py:53
  42.4 5.2 %gather_fusion.1 = bf16[384,2,8,128]{3,2,1,0:T(8,128)(2,1)S(1)} fusion(bf16[128,2,8,8,128]{4,3,2,1,0:T(8,128)(2,1)} %param.12, s32[384]{0:T(512)S(1)} %reshape.354), kind=kCustom, calls=%fused_computation.1 | custom fusion | bytes 3148800 | tf_op jit(solution)/shard_map/gather | solution.py:97
  47.6 8.0 %broadcast_in_dim.202 = bf16[16,8,2,12,2,8,128]{6,5,4,3,2,1,0:T(8,128)(2,1)} broadcast(bf16[16,2,12,2,8,128]{5,4,3,2,1,0:T(8,128)(2,1)S(1)} %bitcast.169), dimensions={0,2,3,4,5,6} | broadcast | bytes 14155776 | tf_op jit(solution)/shard_map/broadcast_in_dim | solution.py:99
  55.6 11.8 %all-to-all-start.2 = ((bf16[128,1,2,12,2,8,128]{6,5,4,3,2,1,0:T(8,128)(2,1)}), bf16[128,1,2,12,2,8,128]{6,5,4,3,2,1,0:T(8,128)(2,1)}, u32[]{:S(2)}, u32[]{:S(2)}) async-start(bf16[128,1,2,12,2,8,128]{6,5,4,3,2,1,0:T(8,128)(2,1)} %bitcast.166), calls=%async_computation.2 | async-start | bytes 25165824 | tf_op jit(solution)/shard_map/all_to_all | solution.py:102
  67.6 133.7 %while.41 = (s32[]{:T(128)}, f32[2,1024,1]{1,0,2:T(2,128)S(1)}, f32[2,1024,1]{1,0,2:T(2,128)S(1)}, f32[2,1024,128]{2,1,0:T(8,128)S(1)}, bf16[2,8192,128]{2,1,0:T...) while((s32[]{:T(128)}, f32[2,1024,1]{1,0,2:T(2,128)S(1)}, ...), condition=%wide.region_3.4_spmd.clone.clone, body=%wide.region_0.3_spmd.clone.clone.sunk | while | flops 1102876672 | bytes 32655572 | solution.py:81
  68.3 6.0 %fusion.98 = (f32[2,1024]{1,0:T(2,128)S(1)}, f32[1024,1024,2]{1,0,2:T(8,128)}) fusion(pred[1024,1024]{0,1:T(8,128)(4,1)S(1)} %broadcast_compare_fusion.4, bf16[1024,2,128]{2,0,1:T(8,128)(2,1)S(1)} %get-tuple-element.746, bf16[2,8192,128]{2,1,0:T(8,128)(2,1)} %get-tuple-element.745, s32[]{:T(128)S(6)} %select_n.332), kind=kOutput, calls=%fused_computation.32.clone.1 | convolution fusion | flops 543160320 | bytes 10231812 | tf_op jit(solution)/shard_map/while/body/eval_jaxpr/qpd,kd->pqk/dot_general | solution.py:69
  78.9 5.3 %fusion.101 = f32[2,1024,128]{2,1,0:T(8,128)S(1)} fusion(f32[1024,1024,2]{1,0,2:T(8,128)} %get-tuple-element.715, f32[2,1024]{1,0:T(2,128)S(1)} %bitcast.176, pred[1024,1024]{0,1:T(8,128)(4,1)S(1)} %broadcast_compare_fusion.4, f32[2,1024,128]{2,1,0:T(8,128)S(1)} %get-tuple-element.732, f32[2,1024]{1,0:T(2,128)S(1)} %get-tuple-element.716, ...), kind=kOutput, calls=%fused_computation.38.clone.1 | convolution fusion | flops 548143104 | bytes 11812873 | tf_op jit(solution)/shard_map/while/body/eval_jaxpr/pqk,kd->pqd/dot_general | solution.py:75
  85.0 6.0 %fusion.98 = (f32[2,1024]{1,0:T(2,128)S(1)}, f32[1024,1024,2]{1,0,2:T(8,128)}) fusion(pred[1024,1024]{0,1:T(8,128)(4,1)S(1)} %broadcast_compare_fusion.4, bf16[1024,2,128]{2,0,1:T(8,128)(2,1)S(1)} %get-tuple-element.746, bf16[2,8192,128]{2,1,0:T(8,128)(2,1)} %get-tuple-element.745, s32[]{:T(128)S(6)} %select_n.332), kind=kOutput, calls=%fused_computation.32.clone.1 | convolution fusion | flops 543160320 | bytes 10231812 | tf_op jit(solution)/shard_map/while/body/eval_jaxpr/qpd,kd->pqk/dot_general | solution.py:69
  95.6 5.3 %fusion.101 = f32[2,1024,128]{2,1,0:T(8,128)S(1)} fusion(f32[1024,1024,2]{1,0,2:T(8,128)} %get-tuple-element.715, f32[2,1024]{1,0:T(2,128)S(1)} %bitcast.176, pred[1024,1024]{0,1:T(8,128)(4,1)S(1)} %broadcast_compare_fusion.4, f32[2,1024,128]{2,1,0:T(8,128)S(1)} %get-tuple-element.732, f32[2,1024]{1,0:T(2,128)S(1)} %get-tuple-element.716, ...), kind=kOutput, calls=%fused_computation.38.clone.1 | convolution fusion | flops 548143104 | bytes 11812873 | tf_op jit(solution)/shard_map/while/body/eval_jaxpr/pqk,kd->pqd/dot_general | solution.py:75
  101.7 6.0 %fusion.98 = (f32[2,1024]{1,0:T(2,128)S(1)}, f32[1024,1024,2]{1,0,2:T(8,128)}) fusion(pred[1024,1024]{0,1:T(8,128)(4,1)S(1)} %broadcast_compare_fusion.4, bf16[1024,2,128]{2,0,1:T(8,128)(2,1)S(1)} %get-tuple-element.746, bf16[2,8192,128]{2,1,0:T(8,128)(2,1)} %get-tuple-element.745, s32[]{:T(128)S(6)} %select_n.332), kind=kOutput, calls=%fused_computation.32.clone.1 | convolution fusion | flops 543160320 | bytes 10231812 | tf_op jit(solution)/shard_map/while/body/eval_jaxpr/qpd,kd->pqk/dot_general | solution.py:69
  112.3 5.3 %fusion.101 = f32[2,1024,128]{2,1,0:T(8,128)S(1)} fusion(f32[1024,1024,2]{1,0,2:T(8,128)} %get-tuple-element.715, f32[2,1024]{1,0:T(2,128)S(1)} %bitcast.176, pred[1024,1024]{0,1:T(8,128)(4,1)S(1)} %broadcast_compare_fusion.4, f32[2,1024,128]{2,1,0:T(8,128)S(1)} %get-tuple-element.732, f32[2,1024]{1,0:T(2,128)S(1)} %get-tuple-element.716, ...), kind=kOutput, calls=%fused_computation.38.clone.1 | convolution fusion | flops 548143104 | bytes 11812873 | tf_op jit(solution)/shard_map/while/body/eval_jaxpr/pqk,kd->pqd/dot_general | solution.py:75
  118.4 6.0 %fusion.98 = (f32[2,1024]{1,0:T(2,128)S(1)}, f32[1024,1024,2]{1,0,2:T(8,128)}) fusion(pred[1024,1024]{0,1:T(8,128)(4,1)S(1)} %broadcast_compare_fusion.4, bf16[1024,2,128]{2,0,1:T(8,128)(2,1)S(1)} %get-tuple-element.746, bf16[2,8192,128]{2,1,0:T(8,128)(2,1)} %get-tuple-element.745, s32[]{:T(128)S(6)} %select_n.332), kind=kOutput, calls=%fused_computation.32.clone.1 | convolution fusion | flops 543160320 | bytes 10231812 | tf_op jit(solution)/shard_map/while/body/eval_jaxpr/qpd,kd->pqk/dot_general | solution.py:69
  129.1 5.3 %fusion.101 = f32[2,1024,128]{2,1,0:T(8,128)S(1)} fusion(f32[1024,1024,2]{1,0,2:T(8,128)} %get-tuple-element.715, f32[2,1024]{1,0:T(2,128)S(1)} %bitcast.176, pred[1024,1024]{0,1:T(8,128)(4,1)S(1)} %broadcast_compare_fusion.4, f32[2,1024,128]{2,1,0:T(8,128)S(1)} %get-tuple-element.732, f32[2,1024]{1,0:T(2,128)S(1)} %get-tuple-element.716, ...), kind=kOutput, calls=%fused_computation.38.clone.1 | convolution fusion | flops 548143104 | bytes 11812873 | tf_op jit(solution)/shard_map/while/body/eval_jaxpr/pqk,kd->pqd/dot_general | solution.py:75
  135.1 6.0 %fusion.98 = (f32[2,1024]{1,0:T(2,128)S(1)}, f32[1024,1024,2]{1,0,2:T(8,128)}) fusion(pred[1024,1024]{0,1:T(8,128)(4,1)S(1)} %broadcast_compare_fusion.4, bf16[1024,2,128]{2,0,1:T(8,128)(2,1)S(1)} %get-tuple-element.746, bf16[2,8192,128]{2,1,0:T(8,128)(2,1)} %get-tuple-element.745, s32[]{:T(128)S(6)} %select_n.332), kind=kOutput, calls=%fused_computation.32.clone.1 | convolution fusion | flops 543160320 | bytes 10231812 | tf_op jit(solution)/shard_map/while/body/eval_jaxpr/qpd,kd->pqk/dot_general | solution.py:69
  145.8 5.3 %fusion.101 = f32[2,1024,128]{2,1,0:T(8,128)S(1)} fusion(f32[1024,1024,2]{1,0,2:T(8,128)} %get-tuple-element.715, f32[2,1024]{1,0:T(2,128)S(1)} %bitcast.176, pred[1024,1024]{0,1:T(8,128)(4,1)S(1)} %broadcast_compare_fusion.4, f32[2,1024,128]{2,1,0:T(8,128)S(1)} %get-tuple-element.732, f32[2,1024]{1,0:T(2,128)S(1)} %get-tuple-element.716, ...), kind=kOutput, calls=%fused_computation.38.clone.1 | convolution fusion | flops 548143104 | bytes 11812873 | tf_op jit(solution)/shard_map/while/body/eval_jaxpr/pqk,kd->pqd/dot_general | solution.py:75
  151.9 6.0 %fusion.98 = (f32[2,1024]{1,0:T(2,128)S(1)}, f32[1024,1024,2]{1,0,2:T(8,128)}) fusion(pred[1024,1024]{0,1:T(8,128)(4,1)S(1)} %broadcast_compare_fusion.4, bf16[1024,2,128]{2,0,1:T(8,128)(2,1)S(1)} %get-tuple-element.746, bf16[2,8192,128]{2,1,0:T(8,128)(2,1)} %get-tuple-element.745, s32[]{:T(128)S(6)} %select_n.332), kind=kOutput, calls=%fused_computation.32.clone.1 | convolution fusion | flops 543160320 | bytes 10231812 | tf_op jit(solution)/shard_map/while/body/eval_jaxpr/qpd,kd->pqk/dot_general | solution.py:69
  162.5 5.3 %fusion.101 = f32[2,1024,128]{2,1,0:T(8,128)S(1)} fusion(f32[1024,1024,2]{1,0,2:T(8,128)} %get-tuple-element.715, f32[2,1024]{1,0:T(2,128)S(1)} %bitcast.176, pred[1024,1024]{0,1:T(8,128)(4,1)S(1)} %broadcast_compare_fusion.4, f32[2,1024,128]{2,1,0:T(8,128)S(1)} %get-tuple-element.732, f32[2,1024]{1,0:T(2,128)S(1)} %get-tuple-element.716, ...), kind=kOutput, calls=%fused_computation.38.clone.1 | convolution fusion | flops 548143104 | bytes 11812873 | tf_op jit(solution)/shard_map/while/body/eval_jaxpr/pqk,kd->pqd/dot_general | solution.py:75
  168.6 6.0 %fusion.98 = (f32[2,1024]{1,0:T(2,128)S(1)}, f32[1024,1024,2]{1,0,2:T(8,128)}) fusion(pred[1024,1024]{0,1:T(8,128)(4,1)S(1)} %broadcast_compare_fusion.4, bf16[1024,2,128]{2,0,1:T(8,128)(2,1)S(1)} %get-tuple-element.746, bf16[2,8192,128]{2,1,0:T(8,128)(2,1)} %get-tuple-element.745, s32[]{:T(128)S(6)} %select_n.332), kind=kOutput, calls=%fused_computation.32.clone.1 | convolution fusion | flops 543160320 | bytes 10231812 | tf_op jit(solution)/shard_map/while/body/eval_jaxpr/qpd,kd->pqk/dot_general | solution.py:69
  179.2 5.3 %fusion.101 = f32[2,1024,128]{2,1,0:T(8,128)S(1)} fusion(f32[1024,1024,2]{1,0,2:T(8,128)} %get-tuple-element.715, f32[2,1024]{1,0:T(2,128)S(1)} %bitcast.176, pred[1024,1024]{0,1:T(8,128)(4,1)S(1)} %broadcast_compare_fusion.4, f32[2,1024,128]{2,1,0:T(8,128)S(1)} %get-tuple-element.732, f32[2,1024]{1,0:T(2,128)S(1)} %get-tuple-element.716, ...), kind=kOutput, calls=%fused_computation.38.clone.1 | convolution fusion | flops 548143104 | bytes 11812873 | tf_op jit(solution)/shard_map/while/body/eval_jaxpr/pqk,kd->pqd/dot_general | solution.py:75
  185.3 6.0 %fusion.98 = (f32[2,1024]{1,0:T(2,128)S(1)}, f32[1024,1024,2]{1,0,2:T(8,128)}) fusion(pred[1024,1024]{0,1:T(8,128)(4,1)S(1)} %broadcast_compare_fusion.4, bf16[1024,2,128]{2,0,1:T(8,128)(2,1)S(1)} %get-tuple-element.746, bf16[2,8192,128]{2,1,0:T(8,128)(2,1)} %get-tuple-element.745, s32[]{:T(128)S(6)} %select_n.332), kind=kOutput, calls=%fused_computation.32.clone.1 | convolution fusion | flops 543160320 | bytes 10231812 | tf_op jit(solution)/shard_map/while/body/eval_jaxpr/qpd,kd->pqk/dot_general | solution.py:69
  195.9 5.3 %fusion.101 = f32[2,1024,128]{2,1,0:T(8,128)S(1)} fusion(f32[1024,1024,2]{1,0,2:T(8,128)} %get-tuple-element.715, f32[2,1024]{1,0:T(2,128)S(1)} %bitcast.176, pred[1024,1024]{0,1:T(8,128)(4,1)S(1)} %broadcast_compare_fusion.4, f32[2,1024,128]{2,1,0:T(8,128)S(1)} %get-tuple-element.732, f32[2,1024]{1,0:T(2,128)S(1)} %get-tuple-element.716, ...), kind=kOutput, calls=%fused_computation.38.clone.1 | convolution fusion | flops 548143104 | bytes 11812873 | tf_op jit(solution)/shard_map/while/body/eval_jaxpr/pqk,kd->pqd/dot_general | solution.py:75
  201.3 15.3 %all-to-all-done.2 = bf16[128,1,2,12,2,8,128]{6,5,4,3,2,1,0:T(8,128)(2,1)} async-done(((bf16[128,1,2,12,2,8,128]{6,5,4,3,2,1,0:T(8,128)(2,1)}), bf16[128,1,2,12,2,8,128]{6,5,4,3,2,1,0:T(8,128)(2,1)}, u32[]{:S(2)}, u32[]{:S(2)}) %all-to-all-start.2) | async-done | bytes 12582944 | tf_op jit(solution)/shard_map/all_to_all | solution.py:102
  216.6 11.6 %copy.64 = bf16[2,8,12,2,16,8,128]{6,5,4,3,2,1,0:T(8,128)(2,1)} copy(bf16[2,8,12,2,16,8,128]{6,5,3,2,0,1,4:T(8,128)(2,1)} %bitcast.20) | data formatting | bytes 25165824 | tf_op jit(solution)/shard_map/transpose | solution.py:104
  228.2 105.4 %while.40 = (s32[]{:T(128)}, f32[2,1024,1]{1,0,2:T(2,128)S(1)}, f32[2,1024,1]{1,0,2:T(2,128)S(1)}, f32[2,1024,128]{2,1,0:T(8,128)S(1)}, pred[8,2,12]{2,1,0:T(4,1...) while((s32[]{:T(128)}, f32[2,1024,1]{1,0,2:T(2,128)S(1)}, ...), condition=%wide.region_11.12_spmd, body=%wide.region_8.11_spmd.sunk | while | flops 1652037632 | bytes 45238536 | solution.py:128
  236.2 5.2 %fusion.94 = f32[2,1024,128]{2,1,0:T(8,128)S(1)} fusion(bf16[2,1536,128]{2,1,0:T(8,128)(2,1)S(1)} %bitcast.168, f32[2,1536,1024]{2,1,0:T(8,128)S(1)} %get-tuple-element.701, f32[2,1024]{1,0:T(2,128)S(1)} %bitcast.174, pred[2,1536]{1,0:T(4,128)(4,1)S(1)} %bitcast.172, f32[2,1024,128]{2,1,0:T(8,128)S(1)} %get-tuple-element.768, ...), kind=kOutput, calls=%fused_computation.17.clone.1 | convolution fusion | flops 821559296 | bytes 15485952 | tf_op jit(solution)/shard_map/while/body/eval_jaxpr/pqk,pkd->pqd/dot_general | solution.py:122
  249.3 5.2 %fusion.94 = f32[2,1024,128]{2,1,0:T(8,128)S(1)} fusion(bf16[2,1536,128]{2,1,0:T(8,128)(2,1)S(1)} %bitcast.168, f32[2,1536,1024]{2,1,0:T(8,128)S(1)} %get-tuple-element.701, f32[2,1024]{1,0:T(2,128)S(1)} %bitcast.174, pred[2,1536]{1,0:T(4,128)(4,1)S(1)} %bitcast.172, f32[2,1024,128]{2,1,0:T(8,128)S(1)} %get-tuple-element.768, ...), kind=kOutput, calls=%fused_computation.17.clone.1 | convolution fusion | flops 821559296 | bytes 15485952 | tf_op jit(solution)/shard_map/while/body/eval_jaxpr/pqk,pkd->pqd/dot_general | solution.py:122
  262.5 5.2 %fusion.94 = f32[2,1024,128]{2,1,0:T(8,128)S(1)} fusion(bf16[2,1536,128]{2,1,0:T(8,128)(2,1)S(1)} %bitcast.168, f32[2,1536,1024]{2,1,0:T(8,128)S(1)} %get-tuple-element.701, f32[2,1024]{1,0:T(2,128)S(1)} %bitcast.174, pred[2,1536]{1,0:T(4,128)(4,1)S(1)} %bitcast.172, f32[2,1024,128]{2,1,0:T(8,128)S(1)} %get-tuple-element.768, ...), kind=kOutput, calls=%fused_computation.17.clone.1 | convolution fusion | flops 821559296 | bytes 15485952 | tf_op jit(solution)/shard_map/while/body/eval_jaxpr/pqk,pkd->pqd/dot_general | solution.py:122
  275.7 5.2 %fusion.94 = f32[2,1024,128]{2,1,0:T(8,128)S(1)} fusion(bf16[2,1536,128]{2,1,0:T(8,128)(2,1)S(1)} %bitcast.168, f32[2,1536,1024]{2,1,0:T(8,128)S(1)} %get-tuple-element.701, f32[2,1024]{1,0:T(2,128)S(1)} %bitcast.174, pred[2,1536]{1,0:T(4,128)(4,1)S(1)} %bitcast.172, f32[2,1024,128]{2,1,0:T(8,128)S(1)} %get-tuple-element.768, ...), kind=kOutput, calls=%fused_computation.17.clone.1 | convolution fusion | flops 821559296 | bytes 15485952 | tf_op jit(solution)/shard_map/while/body/eval_jaxpr/pqk,pkd->pqd/dot_general | solution.py:122
  288.9 5.2 %fusion.94 = f32[2,1024,128]{2,1,0:T(8,128)S(1)} fusion(bf16[2,1536,128]{2,1,0:T(8,128)(2,1)S(1)} %bitcast.168, f32[2,1536,1024]{2,1,0:T(8,128)S(1)} %get-tuple-element.701, f32[2,1024]{1,0:T(2,128)S(1)} %bitcast.174, pred[2,1536]{1,0:T(4,128)(4,1)S(1)} %bitcast.172, f32[2,1024,128]{2,1,0:T(8,128)S(1)} %get-tuple-element.768, ...), kind=kOutput, calls=%fused_computation.17.clone.1 | convolution fusion | flops 821559296 | bytes 15485952 | tf_op jit(solution)/shard_map/while/body/eval_jaxpr/pqk,pkd->pqd/dot_general | solution.py:122
  302.1 5.2 %fusion.94 = f32[2,1024,128]{2,1,0:T(8,128)S(1)} fusion(bf16[2,1536,128]{2,1,0:T(8,128)(2,1)S(1)} %bitcast.168, f32[2,1536,1024]{2,1,0:T(8,128)S(1)} %get-tuple-element.701, f32[2,1024]{1,0:T(2,128)S(1)} %bitcast.174, pred[2,1536]{1,0:T(4,128)(4,1)S(1)} %bitcast.172, f32[2,1024,128]{2,1,0:T(8,128)S(1)} %get-tuple-element.768, ...), kind=kOutput, calls=%fused_computation.17.clone.1 | convolution fusion | flops 821559296 | bytes 15485952 | tf_op jit(solution)/shard_map/while/body/eval_jaxpr/pqk,pkd->pqd/dot_general | solution.py:122
  315.2 5.2 %fusion.94 = f32[2,1024,128]{2,1,0:T(8,128)S(1)} fusion(bf16[2,1536,128]{2,1,0:T(8,128)(2,1)S(1)} %bitcast.168, f32[2,1536,1024]{2,1,0:T(8,128)S(1)} %get-tuple-element.701, f32[2,1024]{1,0:T(2,128)S(1)} %bitcast.174, pred[2,1536]{1,0:T(4,128)(4,1)S(1)} %bitcast.172, f32[2,1024,128]{2,1,0:T(8,128)S(1)} %get-tuple-element.768, ...), kind=kOutput, calls=%fused_computation.17.clone.1 | convolution fusion | flops 821559296 | bytes 15485952 | tf_op jit(solution)/shard_map/while/body/eval_jaxpr/pqk,pkd->pqd/dot_general | solution.py:122
  334.8 23.9 %all_to_all.55 = bf16[16,64,256]{2,1,0:T(8,128)(2,1)S(1)} all-to-all(bf16[16,64,256]{2,1,0:T(8,128)(2,1)S(1)} %reshape.344), channel_id=1, replica_groups=mesh['seq'=16,'ctx'=8] {'seq'}, dimensions={0} | all-to-all | bytes 1048576 | tf_op jit(solution)/shard_map/all_to_all | solution.py:132
  (174 shorter events, 131.6 us)
Async XLA Ops:
  6.5 1.0 copy-start
  6.5 26.9 %copy-start.2 = (s32[1024]{0:T(1024)S(1)}, s32[1024]{0:T(1024)}, u32[]{:S(2)}) copy-start(s32[1024]{0:T(1024)} %param.15) | copy-start | bytes 12292
  6.5 61.0 %all-gather.2.cloned.1.call-start = ((), (), s32[]{:S(2)}) async-start(), calls=%async_computation.4 | async-start | bytes 4718592 | tf_op jit(solution)/shard_map/all_gather | solution.py:63
  28.3 19.2 %all-to-all-start.1 = ((bf16[64,16,256]{2,0,1:T(8,128)(2,1)}), bf16[64,16,256]{2,0,1:T(8,128)(2,1)S(1)}, u32[]{:S(2)}, u32[]{:S(2)}) async-start(bf16[64,16,256]{2,0,1:T(8,128)(2,1)} %bitcast.118), calls=%async_computation.1 | async-start | bytes 1048576 | tf_op jit(solution)/shard_map/all_to_all | solution.py:49
  55.6 161.0 %all-to-all-start.2 = ((bf16[128,1,2,12,2,8,128]{6,5,4,3,2,1,0:T(8,128)(2,1)}), bf16[128,1,2,12,2,8,128]{6,5,4,3,2,1,0:T(8,128)(2,1)}, u32[]{:S(2)}, u32[]{:S(2)}) async-start(bf16[128,1,2,12,2,8,128]{6,5,4,3,2,1,0:T(8,128)(2,1)} %bitcast.166), calls=%async_computation.2 | async-start | bytes 25165824 | tf_op jit(solution)/shard_map/all_to_all | solution.py:102
  333.6 26.0 %copy-start.1 = (bf16[2,64,1024]{2,1,0:T(8,128)(2,1)S(1)}, bf16[2,64,1024]{2,1,0:T(8,128)(2,1)}, u32[]{:S(2)}) copy-start(bf16[2,64,1024]{2,1,0:T(8,128)(2,1)} %param.11) | copy-start | bytes 786436
Sparse Core Ops, SparseCore 0:
  26.6 30.3 all-gather.1
where the time goes:
time: 367 us; the launch traced here: 366 us
  matrix products  154 us (42%)
  other arithmetic  76.5 us (21%)
  local copies, waits for them, and re-layouts  48.3 us (13%)
  blocking collectives  41.8 us (11%)
  starting transfers between devices  15.3 us (4%)
  waiting for transfers between devices  15.3 us (4%)
  between operations  13.6 us (4%)
    reduce_sum x16, other arithmetic, online_update(): new_sum = running_sum * fading + jnp.sum(weights, axis=2, keepdims=True)  64.7 us
    dot_general x8, matrix products, visit(): jnp.einsum('qpd,kd->pqk', own_queries, shard_kv[0], preferred_element_typ...  47.7 us
    dot_general x8, matrix products, stretch_mix(): jnp.einsum('pqk,kd->pqd', rounded, shard_kv[1], preferred_element_type=jn...  42.8 us
    dot_general x8, matrix products, block_mix(): jnp.einsum('pqk,pkd->pqd', rounded, block_values, preferred_element_type=...  41.2 us
    all_to_all x1, blocking collectives, on_device(): lax.all_to_all(outgoing, 'seq', split_axis=0, concat_axis=2, tiled=True)  23.9 us
    dot_general x8, matrix products, visit(): jnp.einsum('qpd,pkd->pqk', own_queries, block_keys, preferred_element_typ...  22.7 us
    all_to_all x1, blocking collectives, on_device(): lax.all_to_all(widened_kv, 'seq', split_axis=2, concat_axis=1, tiled=True)  17.9 us
    all_to_all x1, waiting for transfers between devices, on_device(): lax.all_to_all(widened, ('seq', 'ctx'), split_axis=0, concat_axis=1, tile...  15.3 us
  transfers between devices with their start and end apart: 3, of which 1 were waited for; matrix products, arithmetic and copies ran while one was open for 43% of the time, Pallas kernels for 0%

commit v1 on v0

--- a/solution.py
+++ b/solution.py
@@ -50,9 +50,10 @@
         sent_queries, "seq", split_axis=1, concat_axis=0, tiled=True
     ).reshape(query_rows, per_device, HD)
     widened_kv = jnp.repeat(stretch_kv.reshape(2, tok_rows, KVH, HD), n_seq // KVH, axis=2)
-    own_kv = lax.all_to_all(widened_kv, "seq", split_axis=2, concat_axis=1, tiled=True).reshape(
-        2, query_rows, HD
-    )
+    own_kv = jnp.concatenate(
+        lax.all_to_all(jnp.stack(jnp.split(widened_kv, lax.axis_size("seq"), axis=2)), "seq", 0, 0),
+        axis=1,
+    ).reshape(2, query_rows, HD)
     row_index = jnp.arange(query_rows, dtype=jnp.int32)
     query_position = stretch_positions(row_index, ctx_index, tok_rows, n_ctx)
     start_carry = (

time: 367 us -> 368 us (level)
  other arithmetic: 76.5 us -> 57.5 us
  waiting for transfers between devices: 15.3 us -> 29.8 us
    reduce_sum x16, other arithmetic: 64.7 us -> 45.7 us  [online_update(): new_sum = running_sum * fading + jnp.sum(weights, axis=2, keepdims=True)]
    all_to_all x1, waiting for transfers between devices: 15.3 us -> 29.7 us  [on_device(): lax.all_to_all(widened, ('seq', 'ctx'), split_axis=0, concat_axis=1, tile...]
  transfers between devices with their start and end apart: 3 -> 3, of which waited for: 1 -> 1; matrix products, arithmetic and copies ran while one was open for 43% -> 38% of each run, Pallas kernels for 0% -> 0%
where the time goes in v1:
time: 368 us; the launch traced here: 367 us
  matrix products  156 us (42%)
  other arithmetic  57.5 us (16%)
  local copies, waits for them, and re-layouts  51.7 us (14%)
  blocking collectives  42 us (11%)
  waiting for transfers between devices  29.8 us (8%)
  starting transfers between devices  15.3 us (4%)
  between operations  13.7 us (4%)
    dot_general x8, matrix products, visit(): jnp.einsum('qpd,kd->pqk', own_queries, shard_kv[0], preferred_element_typ...  47.7 us
    reduce_sum x16, other arithmetic, online_update(): new_sum = running_sum * fading + jnp.sum(weights, axis=2, keepdims=True)  45.7 us
    dot_general x8, matrix products, stretch_mix(): jnp.einsum('pqk,kd->pqd', rounded, shard_kv[1], preferred_element_type=jn...  44 us
    dot_general x8, matrix products, block_mix(): jnp.einsum('pqk,pkd->pqd', rounded, block_values, preferred_element_type=...  41.1 us
    all_to_all x1, waiting for transfers between devices, on_device(): lax.all_to_all(widened, ('seq', 'ctx'), split_axis=0, concat_axis=1, tile...  29.7 us
    all_to_all x1, blocking collectives, on_device(): lax.all_to_all(outgoing, 'seq', split_axis=0, concat_axis=2, tiled=True)  24.1 us
    dot_general x8, matrix products, visit(): jnp.einsum('qpd,pkd->pqk', own_queries, block_keys, preferred_element_typ...  22.7 us
    all_to_all x1, blocking collectives, on_device(): lax.all_to_all(jnp.stack(jnp.split(widened_kv, lax.axis_size('seq'), axis...  17.9 us
  transfers between devices with their start and end apart: 3, of which 1 were waited for; matrix products, arithmetic and copies ran while one was open for 38% of the time, Pallas kernels for 0%

profile of v1, /device:TPU:9, one launch (start us, length us, event | category | flops | bytes accessed | tf_op | source)
XLA Modules:
  0.0 366.7 jit_solution(12547652169963911107)
XLA Ops:
  7.9 17.9 %all_to_all.44 = bf16[16,2,64,1,128]{4,2,1,3,0:T(8,128)(2,1)S(1)} all-to-all(bf16[16,2,64,1,128]{4,2,1,3,0:T(8,128)(2,1)S(1)} %fusion.60), channel_id=1, replica_groups=mesh['seq'=16,'ctx'=8] {'seq'}, dimensions={0} | all-to-all | bytes 1048576 | tf_op jit(solution)/shard_map/all_to_all | solution.py:54
  42.7 5.2 %gather_fusion.1 = bf16[384,2,8,128]{3,2,1,0:T(8,128)(2,1)S(1)} fusion(bf16[128,2,8,8,128]{4,3,2,1,0:T(8,128)(2,1)} %param.12, s32[384]{0:T(512)S(1)} %reshape.353), kind=kCustom, calls=%fused_computation.1 | custom fusion | bytes 3148800 | tf_op jit(solution)/shard_map/gather | solution.py:98
  47.8 8.0 %broadcast_in_dim.202 = bf16[16,8,2,12,2,8,128]{6,5,4,3,2,1,0:T(8,128)(2,1)} broadcast(bf16[16,2,12,2,8,128]{5,4,3,2,1,0:T(8,128)(2,1)S(1)} %bitcast.231), dimensions={0,2,3,4,5,6} | broadcast | bytes 14155776 | tf_op jit(solution)/shard_map/broadcast_in_dim | solution.py:100
  55.8 11.8 %all-to-all-start.2 = ((bf16[128,1,2,12,2,8,128]{6,5,4,3,2,1,0:T(8,128)(2,1)}), bf16[128,1,2,12,2,8,128]{6,5,4,3,2,1,0:T(8,128)(2,1)}, u32[]{:S(2)}, u32[]{:S(2)}) async-start(bf16[128,1,2,12,2,8,128]{6,5,4,3,2,1,0:T(8,128)(2,1)} %bitcast.228), calls=%async_computation.2 | async-start | bytes 25165824 | tf_op jit(solution)/shard_map/all_to_all | solution.py:103
  67.8 119.3 %while.41 = (s32[]{:T(128)}, f32[2,1024,1]{1,0,2:T(2,128)S(1)}, f32[2,1024,1]{1,0,2:T(2,128)S(1)}, f32[2,1024,128]{2,1,0:T(8,128)S(1)}, bf16[2,8192,128]{2,1,0:T...) while((s32[]{:T(128)}, f32[2,1024,1]{1,0,2:T(2,128)S(1)}, ...), condition=%wide.region_3.4_spmd.clone.clone, body=%wide.region_0.3_spmd.clone.clone.sunk | while | flops 1102876672 | bytes 66210024 | solution.py:82
  68.5 6.0 %fusion.114 = (f32[2,1024]{1,0:T(2,128)S(1)}, f32[1024,1024,2]{1,0,2:T(8,128)}) fusion(pred[1024,1024]{0,1:T(8,128)(4,1)S(1)} %broadcast_compare_fusion.4, bf16[1024,2,128]{2,0,1:T(8,128)(2,1)S(1)} %get-tuple-element.746, bf16[2,8192,128]{2,1,0:T(8,128)(2,1)} %get-tuple-element.745, s32[]{:T(128)S(6)} %select_n.332), kind=kOutput, calls=%fused_computation.32.clone.1 | convolution fusion | flops 543160320 | bytes 10231812 | tf_op jit(solution)/shard_map/while/body/eval_jaxpr/qpd,kd->pqk/dot_general | solution.py:70
  74.5 5.5 %fusion.117 = f32[2,1024,128]{2,1,0:T(8,128)S(1)} fusion(f32[1024,1024,2]{1,0,2:T(8,128)} %get-tuple-element.715, f32[2,1024]{1,0:T(2,128)S(1)} %bitcast.237, pred[1024,1024]{0,1:T(8,128)(4,1)S(1)} %broadcast_compare_fusion.4, f32[2,1024,128]{2,1,0:T(8,128)S(1)} %get-tuple-element.732, f32[2,1024]{1,0:T(2,128)S(1)} %get-tuple-element.716, ...), kind=kOutput, calls=%fused_computation.38.clone.1 | convolution fusion | flops 548143104 | bytes 11812873 | tf_op jit(solution)/shard_map/while/body/eval_jaxpr/pqk,kd->pqd/dot_general | solution.py:76
  83.4 6.0 %fusion.114 = (f32[2,1024]{1,0:T(2,128)S(1)}, f32[1024,1024,2]{1,0,2:T(8,128)}) fusion(pred[1024,1024]{0,1:T(8,128)(4,1)S(1)} %broadcast_compare_fusion.4, bf16[1024,2,128]{2,0,1:T(8,128)(2,1)S(1)} %get-tuple-element.746, bf16[2,8192,128]{2,1,0:T(8,128)(2,1)} %get-tuple-element.745, s32[]{:T(128)S(6)} %select_n.332), kind=kOutput, calls=%fused_computation.32.clone.1 | convolution fusion | flops 543160320 | bytes 10231812 | tf_op jit(solution)/shard_map/while/body/eval_jaxpr/qpd,kd->pqk/dot_general | solution.py:70
  89.4 5.5 %fusion.117 = f32[2,1024,128]{2,1,0:T(8,128)S(1)} fusion(f32[1024,1024,2]{1,0,2:T(8,128)} %get-tuple-element.715, f32[2,1024]{1,0:T(2,128)S(1)} %bitcast.237, pred[1024,1024]{0,1:T(8,128)(4,1)S(1)} %broadcast_compare_fusion.4, f32[2,1024,128]{2,1,0:T(8,128)S(1)} %get-tuple-element.732, f32[2,1024]{1,0:T(2,128)S(1)} %get-tuple-element.716, ...), kind=kOutput, calls=%fused_computation.38.clone.1 | convolution fusion | flops 548143104 | bytes 11812873 | tf_op jit(solution)/shard_map/while/body/eval_jaxpr/pqk,kd->pqd/dot_general | solution.py:76
  98.4 6.0 %fusion.114 = (f32[2,1024]{1,0:T(2,128)S(1)}, f32[1024,1024,2]{1,0,2:T(8,128)}) fusion(pred[1024,1024]{0,1:T(8,128)(4,1)S(1)} %broadcast_compare_fusion.4, bf16[1024,2,128]{2,0,1:T(8,128)(2,1)S(1)} %get-tuple-element.746, bf16[2,8192,128]{2,1,0:T(8,128)(2,1)} %get-tuple-element.745, s32[]{:T(128)S(6)} %select_n.332), kind=kOutput, calls=%fused_computation.32.clone.1 | convolution fusion | flops 543160320 | bytes 10231812 | tf_op jit(solution)/shard_map/while/body/eval_jaxpr/qpd,kd->pqk/dot_general | solution.py:70
  104.3 5.5 %fusion.117 = f32[2,1024,128]{2,1,0:T(8,128)S(1)} fusion(f32[1024,1024,2]{1,0,2:T(8,128)} %get-tuple-element.715, f32[2,1024]{1,0:T(2,128)S(1)} %bitcast.237, pred[1024,1024]{0,1:T(8,128)(4,1)S(1)} %broadcast_compare_fusion.4, f32[2,1024,128]{2,1,0:T(8,128)S(1)} %get-tuple-element.732, f32[2,1024]{1,0:T(2,128)S(1)} %get-tuple-element.716, ...), kind=kOutput, calls=%fused_computation.38.clone.1 | convolution fusion | flops 548143104 | bytes 11812873 | tf_op jit(solution)/shard_map/while/body/eval_jaxpr/pqk,kd->pqd/dot_general | solution.py:76
  113.3 6.0 %fusion.114 = (f32[2,1024]{1,0:T(2,128)S(1)}, f32[1024,1024,2]{1,0,2:T(8,128)}) fusion(pred[1024,1024]{0,1:T(8,128)(4,1)S(1)} %broadcast_compare_fusion.4, bf16[1024,2,128]{2,0,1:T(8,128)(2,1)S(1)} %get-tuple-element.746, bf16[2,8192,128]{2,1,0:T(8,128)(2,1)} %get-tuple-element.745, s32[]{:T(128)S(6)} %select_n.332), kind=kOutput, calls=%fused_computation.32.clone.1 | convolution fusion | flops 543160320 | bytes 10231812 | tf_op jit(solution)/shard_map/while/body/eval_jaxpr/qpd,kd->pqk/dot_general | solution.py:70
  119.3 5.5 %fusion.117 = f32[2,1024,128]{2,1,0:T(8,128)S(1)} fusion(f32[1024,1024,2]{1,0,2:T(8,128)} %get-tuple-element.715, f32[2,1024]{1,0:T(2,128)S(1)} %bitcast.237, pred[1024,1024]{0,1:T(8,128)(4,1)S(1)} %broadcast_compare_fusion.4, f32[2,1024,128]{2,1,0:T(8,128)S(1)} %get-tuple-element.732, f32[2,1024]{1,0:T(2,128)S(1)} %get-tuple-element.716, ...), kind=kOutput, calls=%fused_computation.38.clone.1 | convolution fusion | flops 548143104 | bytes 11812873 | tf_op jit(solution)/shard_map/while/body/eval_jaxpr/pqk,kd->pqd/dot_general | solution.py:76
  128.2 6.0 %fusion.114 = (f32[2,1024]{1,0:T(2,128)S(1)}, f32[1024,1024,2]{1,0,2:T(8,128)}) fusion(pred[1024,1024]{0,1:T(8,128)(4,1)S(1)} %broadcast_compare_fusion.4, bf16[1024,2,128]{2,0,1:T(8,128)(2,1)S(1)} %get-tuple-element.746, bf16[2,8192,128]{2,1,0:T(8,128)(2,1)} %get-tuple-element.745, s32[]{:T(128)S(6)} %select_n.332), kind=kOutput, calls=%fused_computation.32.clone.1 | convolution fusion | flops 543160320 | bytes 10231812 | tf_op jit(solution)/shard_map/while/body/eval_jaxpr/qpd,kd->pqk/dot_general | solution.py:70
  134.2 5.5 %fusion.117 = f32[2,1024,128]{2,1,0:T(8,128)S(1)} fusion(f32[1024,1024,2]{1,0,2:T(8,128)} %get-tuple-element.715, f32[2,1024]{1,0:T(2,128)S(1)} %bitcast.237, pred[1024,1024]{0,1:T(8,128)(4,1)S(1)} %broadcast_compare_fusion.4, f32[2,1024,128]{2,1,0:T(8,128)S(1)} %get-tuple-element.732, f32[2,1024]{1,0:T(2,128)S(1)} %get-tuple-element.716, ...), kind=kOutput, calls=%fused_computation.38.clone.1 | convolution fusion | flops 548143104 | bytes 11812873 | tf_op jit(solution)/shard_map/while/body/eval_jaxpr/pqk,kd->pqd/dot_general | solution.py:76
  143.1 6.0 %fusion.114 = (f32[2,1024]{1,0:T(2,128)S(1)}, f32[1024,1024,2]{1,0,2:T(8,128)}) fusion(pred[1024,1024]{0,1:T(8,128)(4,1)S(1)} %broadcast_compare_fusion.4, bf16[1024,2,128]{2,0,1:T(8,128)(2,1)S(1)} %get-tuple-element.746, bf16[2,8192,128]{2,1,0:T(8,128)(2,1)} %get-tuple-element.745, s32[]{:T(128)S(6)} %select_n.332), kind=kOutput, calls=%fused_computation.32.clone.1 | convolution fusion | flops 543160320 | bytes 10231812 | tf_op jit(solution)/shard_map/while/body/eval_jaxpr/qpd,kd->pqk/dot_general | solution.py:70
  149.1 5.5 %fusion.117 = f32[2,1024,128]{2,1,0:T(8,128)S(1)} fusion(f32[1024,1024,2]{1,0,2:T(8,128)} %get-tuple-element.715, f32[2,1024]{1,0:T(2,128)S(1)} %bitcast.237, pred[1024,1024]{0,1:T(8,128)(4,1)S(1)} %broadcast_compare_fusion.4, f32[2,1024,128]{2,1,0:T(8,128)S(1)} %get-tuple-element.732, f32[2,1024]{1,0:T(2,128)S(1)} %get-tuple-element.716, ...), kind=kOutput, calls=%fused_computation.38.clone.1 | convolution fusion | flops 548143104 | bytes 11812873 | tf_op jit(solution)/shard_map/while/body/eval_jaxpr/pqk,kd->pqd/dot_general | solution.py:76
  158.0 6.0 %fusion.114 = (f32[2,1024]{1,0:T(2,128)S(1)}, f32[1024,1024,2]{1,0,2:T(8,128)}) fusion(pred[1024,1024]{0,1:T(8,128)(4,1)S(1)} %broadcast_compare_fusion.4, bf16[1024,2,128]{2,0,1:T(8,128)(2,1)S(1)} %get-tuple-element.746, bf16[2,8192,128]{2,1,0:T(8,128)(2,1)} %get-tuple-element.745, s32[]{:T(128)S(6)} %select_n.332), kind=kOutput, calls=%fused_computation.32.clone.1 | convolution fusion | flops 543160320 | bytes 10231812 | tf_op jit(solution)/shard_map/while/body/eval_jaxpr/qpd,kd->pqk/dot_general | solution.py:70
  164.0 5.5 %fusion.117 = f32[2,1024,128]{2,1,0:T(8,128)S(1)} fusion(f32[1024,1024,2]{1,0,2:T(8,128)} %get-tuple-element.715, f32[2,1024]{1,0:T(2,128)S(1)} %bitcast.237, pred[1024,1024]{0,1:T(8,128)(4,1)S(1)} %broadcast_compare_fusion.4, f32[2,1024,128]{2,1,0:T(8,128)S(1)} %get-tuple-element.732, f32[2,1024]{1,0:T(2,128)S(1)} %get-tuple-element.716, ...), kind=kOutput, calls=%fused_computation.38.clone.1 | convolution fusion | flops 548143104 | bytes 11812873 | tf_op jit(solution)/shard_map/while/body/eval_jaxpr/pqk,kd->pqd/dot_general | solution.py:76
  172.9 6.0 %fusion.114 = (f32[2,1024]{1,0:T(2,128)S(1)}, f32[1024,1024,2]{1,0,2:T(8,128)}) fusion(pred[1024,1024]{0,1:T(8,128)(4,1)S(1)} %broadcast_compare_fusion.4, bf16[1024,2,128]{2,0,1:T(8,128)(2,1)S(1)} %get-tuple-element.746, bf16[2,8192,128]{2,1,0:T(8,128)(2,1)} %get-tuple-element.745, s32[]{:T(128)S(6)} %select_n.332), kind=kOutput, calls=%fused_computation.32.clone.1 | convolution fusion | flops 543160320 | bytes 10231812 | tf_op jit(solution)/shard_map/while/body/eval_jaxpr/qpd,kd->pqk/dot_general | solution.py:70
  178.9 5.5 %fusion.117 = f32[2,1024,128]{2,1,0:T(8,128)S(1)} fusion(f32[1024,1024,2]{1,0,2:T(8,128)} %get-tuple-element.715, f32[2,1024]{1,0:T(2,128)S(1)} %bitcast.237, pred[1024,1024]{0,1:T(8,128)(4,1)S(1)} %broadcast_compare_fusion.4, f32[2,1024,128]{2,1,0:T(8,128)S(1)} %get-tuple-element.732, f32[2,1024]{1,0:T(2,128)S(1)} %get-tuple-element.716, ...), kind=kOutput, calls=%fused_computation.38.clone.1 | convolution fusion | flops 548143104 | bytes 11812873 | tf_op jit(solution)/shard_map/while/body/eval_jaxpr/pqk,kd->pqd/dot_general | solution.py:76
  187.1 29.7 %all-to-all-done.2 = bf16[128,1,2,12,2,8,128]{6,5,4,3,2,1,0:T(8,128)(2,1)} async-done(((bf16[128,1,2,12,2,8,128]{6,5,4,3,2,1,0:T(8,128)(2,1)}), bf16[128,1,2,12,2,8,128]{6,5,4,3,2,1,0:T(8,128)(2,1)}, u32[]{:S(2)}, u32[]{:S(2)}) %all-to-all-start.2) | async-done | bytes 12582944 | tf_op jit(solution)/shard_map/all_to_all | solution.py:103
  216.8 11.6 %copy.109 = bf16[2,8,12,2,16,8,128]{6,5,4,3,2,1,0:T(8,128)(2,1)} copy(bf16[2,8,12,2,16,8,128]{6,5,3,2,0,1,4:T(8,128)(2,1)} %bitcast.35) | data formatting | bytes 25165824 | tf_op jit(solution)/shard_map/transpose | solution.py:105
  228.4 105.3 %while.40 = (s32[]{:T(128)}, f32[2,1024,1]{1,0,2:T(2,128)S(1)}, f32[2,1024,1]{1,0,2:T(2,128)S(1)}, f32[2,1024,128]{2,1,0:T(8,128)S(1)}, pred[8,2,12]{2,1,0:T(4,1...) while((s32[]{:T(128)}, f32[2,1024,1]{1,0,2:T(2,128)S(1)}, ...), condition=%wide.region_11.12_spmd, body=%wide.region_8.11_spmd.sunk | while | flops 1652037632 | bytes 45238528 | solution.py:129
  232.9 5.1 %fusion.110 = f32[2,1024,128]{2,1,0:T(8,128)S(1)} fusion(bf16[2,1536,128]{2,1,0:T(8,128)(2,1)S(1)} %bitcast.230, f32[2,1536,1024]{2,1,0:T(8,128)S(1)} %get-tuple-element.701, f32[2,1024]{1,0:T(2,128)S(1)} %bitcast.235, pred[2,1536]{1,0:T(4,128)(4,1)S(1)} %bitcast.233, f32[2,1024,128]{2,1,0:T(8,128)S(1)} %get-tuple-element.768, ...), kind=kOutput, calls=%fused_computation.17.clone.1 | convolution fusion | flops 821559296 | bytes 15485952 | tf_op jit(solution)/shard_map/while/body/eval_jaxpr/pqk,pkd->pqd/dot_general | solution.py:123
  246.0 5.1 %fusion.110 = f32[2,1024,128]{2,1,0:T(8,128)S(1)} fusion(bf16[2,1536,128]{2,1,0:T(8,128)(2,1)S(1)} %bitcast.230, f32[2,1536,1024]{2,1,0:T(8,128)S(1)} %get-tuple-element.701, f32[2,1024]{1,0:T(2,128)S(1)} %bitcast.235, pred[2,1536]{1,0:T(4,128)(4,1)S(1)} %bitcast.233, f32[2,1024,128]{2,1,0:T(8,128)S(1)} %get-tuple-element.768, ...), kind=kOutput, calls=%fused_computation.17.clone.1 | convolution fusion | flops 821559296 | bytes 15485952 | tf_op jit(solution)/shard_map/while/body/eval_jaxpr/pqk,pkd->pqd/dot_general | solution.py:123
  259.2 5.1 %fusion.110 = f32[2,1024,128]{2,1,0:T(8,128)S(1)} fusion(bf16[2,1536,128]{2,1,0:T(8,128)(2,1)S(1)} %bitcast.230, f32[2,1536,1024]{2,1,0:T(8,128)S(1)} %get-tuple-element.701, f32[2,1024]{1,0:T(2,128)S(1)} %bitcast.235, pred[2,1536]{1,0:T(4,128)(4,1)S(1)} %bitcast.233, f32[2,1024,128]{2,1,0:T(8,128)S(1)} %get-tuple-element.768, ...), kind=kOutput, calls=%fused_computation.17.clone.1 | convolution fusion | flops 821559296 | bytes 15485952 | tf_op jit(solution)/shard_map/while/body/eval_jaxpr/pqk,pkd->pqd/dot_general | solution.py:123
  272.4 5.1 %fusion.110 = f32[2,1024,128]{2,1,0:T(8,128)S(1)} fusion(bf16[2,1536,128]{2,1,0:T(8,128)(2,1)S(1)} %bitcast.230, f32[2,1536,1024]{2,1,0:T(8,128)S(1)} %get-tuple-element.701, f32[2,1024]{1,0:T(2,128)S(1)} %bitcast.235, pred[2,1536]{1,0:T(4,128)(4,1)S(1)} %bitcast.233, f32[2,1024,128]{2,1,0:T(8,128)S(1)} %get-tuple-element.768, ...), kind=kOutput, calls=%fused_computation.17.clone.1 | convolution fusion | flops 821559296 | bytes 15485952 | tf_op jit(solution)/shard_map/while/body/eval_jaxpr/pqk,pkd->pqd/dot_general | solution.py:123
  285.5 5.1 %fusion.110 = f32[2,1024,128]{2,1,0:T(8,128)S(1)} fusion(bf16[2,1536,128]{2,1,0:T(8,128)(2,1)S(1)} %bitcast.230, f32[2,1536,1024]{2,1,0:T(8,128)S(1)} %get-tuple-element.701, f32[2,1024]{1,0:T(2,128)S(1)} %bitcast.235, pred[2,1536]{1,0:T(4,128)(4,1)S(1)} %bitcast.233, f32[2,1024,128]{2,1,0:T(8,128)S(1)} %get-tuple-element.768, ...), kind=kOutput, calls=%fused_computation.17.clone.1 | convolution fusion | flops 821559296 | bytes 15485952 | tf_op jit(solution)/shard_map/while/body/eval_jaxpr/pqk,pkd->pqd/dot_general | solution.py:123
  298.7 5.1 %fusion.110 = f32[2,1024,128]{2,1,0:T(8,128)S(1)} fusion(bf16[2,1536,128]{2,1,0:T(8,128)(2,1)S(1)} %bitcast.230, f32[2,1536,1024]{2,1,0:T(8,128)S(1)} %get-tuple-element.701, f32[2,1024]{1,0:T(2,128)S(1)} %bitcast.235, pred[2,1536]{1,0:T(4,128)(4,1)S(1)} %bitcast.233, f32[2,1024,128]{2,1,0:T(8,128)S(1)} %get-tuple-element.768, ...), kind=kOutput, calls=%fused_computation.17.clone.1 | convolution fusion | flops 821559296 | bytes 15485952 | tf_op jit(solution)/shard_map/while/body/eval_jaxpr/pqk,pkd->pqd/dot_general | solution.py:123
  311.9 5.1 %fusion.110 = f32[2,1024,128]{2,1,0:T(8,128)S(1)} fusion(bf16[2,1536,128]{2,1,0:T(8,128)(2,1)S(1)} %bitcast.230, f32[2,1536,1024]{2,1,0:T(8,128)S(1)} %get-tuple-element.701, f32[2,1024]{1,0:T(2,128)S(1)} %bitcast.235, pred[2,1536]{1,0:T(4,128)(4,1)S(1)} %bitcast.233, f32[2,1024,128]{2,1,0:T(8,128)S(1)} %get-tuple-element.768, ...), kind=kOutput, calls=%fused_computation.17.clone.1 | convolution fusion | flops 821559296 | bytes 15485952 | tf_op jit(solution)/shard_map/while/body/eval_jaxpr/pqk,pkd->pqd/dot_general | solution.py:123
  335.0 24.1 %all_to_all.45 = bf16[16,64,256]{2,1,0:T(8,128)(2,1)S(1)} all-to-all(bf16[16,64,256]{2,1,0:T(8,128)(2,1)S(1)} %reshape.343), channel_id=1, replica_groups=mesh['seq'=16,'ctx'=8] {'seq'}, dimensions={0} | all-to-all | bytes 1048576 | tf_op jit(solution)/shard_map/all_to_all | solution.py:133
  (206 shorter events, 116.1 us)
Async XLA Ops:
  6.5 1.0 copy-start
  6.5 27.2 %copy-start.2 = (s32[1024]{0:T(1024)S(1)}, s32[1024]{0:T(1024)}, u32[]{:S(2)}) copy-start(s32[1024]{0:T(1024)} %param.15) | copy-start | bytes 12292
  6.5 61.3 %all-gather.2.cloned.1.call-start = ((), (), s32[]{:S(2)}) async-start(), calls=%async_computation.4 | async-start | bytes 4718592 | tf_op jit(solution)/shard_map/all_gather | solution.py:64
  28.6 19.2 %all-to-all-start.1 = ((bf16[64,16,256]{2,0,1:T(8,128)(2,1)}), bf16[64,16,256]{2,0,1:T(8,128)(2,1)S(1)}, u32[]{:S(2)}, u32[]{:S(2)}) async-start(bf16[64,16,256]{2,0,1:T(8,128)(2,1)} %bitcast.180), calls=%async_computation.1 | async-start | bytes 1048576 | tf_op jit(solution)/shard_map/all_to_all | solution.py:49
  55.8 161.0 %all-to-all-start.2 = ((bf16[128,1,2,12,2,8,128]{6,5,4,3,2,1,0:T(8,128)(2,1)}), bf16[128,1,2,12,2,8,128]{6,5,4,3,2,1,0:T(8,128)(2,1)}, u32[]{:S(2)}, u32[]{:S(2)}) async-start(bf16[128,1,2,12,2,8,128]{6,5,4,3,2,1,0:T(8,128)(2,1)} %bitcast.228), calls=%async_computation.2 | async-start | bytes 25165824 | tf_op jit(solution)/shard_map/all_to_all | solution.py:103
  74.5 5.9 %copy-start.3 = (f32[1024,1024,2]{1,0,2:T(8,128)S(1)}, f32[1024,1024,2]{1,0,2:T(8,128)}, u32[]{:S(2)}) copy-start(f32[1024,1024,2]{1,0,2:T(8,128)} %get-tuple-element.715) | copy-start | bytes 25165828 | tf_op jit(solution)/shard_map/while
  89.4 5.9 %copy-start.3 = (f32[1024,1024,2]{1,0,2:T(8,128)S(1)}, f32[1024,1024,2]{1,0,2:T(8,128)}, u32[]{:S(2)}) copy-start(f32[1024,1024,2]{1,0,2:T(8,128)} %get-tuple-element.715) | copy-start | bytes 25165828 | tf_op jit(solution)/shard_map/while
  104.3 5.9 %copy-start.3 = (f32[1024,1024,2]{1,0,2:T(8,128)S(1)}, f32[1024,1024,2]{1,0,2:T(8,128)}, u32[]{:S(2)}) copy-start(f32[1024,1024,2]{1,0,2:T(8,128)} %get-tuple-element.715) | copy-start | bytes 25165828 | tf_op jit(solution)/shard_map/while
  119.2 5.9 %copy-start.3 = (f32[1024,1024,2]{1,0,2:T(8,128)S(1)}, f32[1024,1024,2]{1,0,2:T(8,128)}, u32[]{:S(2)}) copy-start(f32[1024,1024,2]{1,0,2:T(8,128)} %get-tuple-element.715) | copy-start | bytes 25165828 | tf_op jit(solution)/shard_map/while
  134.2 5.9 %copy-start.3 = (f32[1024,1024,2]{1,0,2:T(8,128)S(1)}, f32[1024,1024,2]{1,0,2:T(8,128)}, u32[]{:S(2)}) copy-start(f32[1024,1024,2]{1,0,2:T(8,128)} %get-tuple-element.715) | copy-start | bytes 25165828 | tf_op jit(solution)/shard_map/while
  149.1 5.9 %copy-start.3 = (f32[1024,1024,2]{1,0,2:T(8,128)S(1)}, f32[1024,1024,2]{1,0,2:T(8,128)}, u32[]{:S(2)}) copy-start(f32[1024,1024,2]{1,0,2:T(8,128)} %get-tuple-element.715) | copy-start | bytes 25165828 | tf_op jit(solution)/shard_map/while
  164.0 5.9 %copy-start.3 = (f32[1024,1024,2]{1,0,2:T(8,128)S(1)}, f32[1024,1024,2]{1,0,2:T(8,128)}, u32[]{:S(2)}) copy-start(f32[1024,1024,2]{1,0,2:T(8,128)} %get-tuple-element.715) | copy-start | bytes 25165828 | tf_op jit(solution)/shard_map/while
  178.9 5.9 %copy-start.3 = (f32[1024,1024,2]{1,0,2:T(8,128)S(1)}, f32[1024,1024,2]{1,0,2:T(8,128)}, u32[]{:S(2)}) copy-start(f32[1024,1024,2]{1,0,2:T(8,128)} %get-tuple-element.715) | copy-start | bytes 25165828 | tf_op jit(solution)/shard_map/while
  333.7 26.2 %copy-start.1 = (bf16[2,64,1024]{2,1,0:T(8,128)(2,1)S(1)}, bf16[2,64,1024]{2,1,0:T(8,128)(2,1)}, u32[]{:S(2)}) copy-start(bf16[2,64,1024]{2,1,0:T(8,128)(2,1)} %param.11) | copy-start | bytes 786436
Sparse Core Ops, SparseCore 0:
  26.8 30.3 all-gather.1
